TPU v7x, 32 devices: a whole 2x2x4 slice. The times are simulated.
32 devices in a mesh: seq: 4 (over z), head: 8 (over y, x, core).
Axes of the slice: x: 2, y: 2, z: 4, core: 2. Of those that a mesh axis runs over, the one named last changes fastest.
Arguments:
- lengths: int32 [16], replicated, may hold values from 128 to 8192, as said below
- page_owner: int32 [384], replicated, may hold values from 0 to 16, as said below
- page_index: int32 [384], replicated, may hold values from 0 to 127, as said below
- page_dest: int32 [384], replicated, may hold values from 0 to 383, as said below
- src_cache: bfloat16 [384, 8, 64, 256], P(('seq', 'head')), may hold values from -8 to 8
- queries: bfloat16 [2, 16, 4096], replicated, may hold values from -8 to 8
- new_kv: bfloat16 [2, 16, 8, 256], replicated, may hold values from -6 to 6
- hidden_in: bfloat16 [2, 16, 4096], P(None, None, ('seq', 'head')), may hold values from -60 to 60
- out_weight: bfloat16 [4096, 4096], P(None, ('seq', 'head')), may hold values from -1.5 to 1.5
- norm_gain: bfloat16 [4096], P(('seq', 'head')), may hold values from 0.099609375 to 1.8984375
- router: bfloat16 [4096, 8], P(('seq', 'head')), may hold values from -0.09375 to 0.09375
- routes: int32 [2, 16, 2], replicated, may hold values from 0 to 7, all different within a row
- w_gate: bfloat16 [8, 4096, 8192], P('seq', None, 'head'), may hold values from -0.09375 to 0.09375
- w_up: bfloat16 [8, 4096, 8192], P('seq', None, 'head'), may hold values from -0.09375 to 0.09375
- w_down: bfloat16 [8, 8192, 4096], P('seq', 'head'), may hold values from -0.0625 to 0.0625
Outputs:
- page_pool: bfloat16 [8, 384, 64, 256], P('head', 'seq')
- mixed: bfloat16 [2, 16, 4096], P(None, None, ('seq', 'head'))
Inputs may be any that keep to these rules, and one draw needn't show every extreme that they name: Each length is at least 128; one equals 8192; the requests' pages, lengths[r] / 64 rounded up for request r, fit into the 384 pages. `page_owner`: request r owns exactly lengths[r] / 64 rounded up source pages; the other pages carry 16. `page_index`: the pages of request r carry 0 to their count minus 1, each once; pages without request carry 0. `page_dest`: A permutation. Slot g belongs to destination group ((g % 384) // 96) + g // 384. Of the 12 pages that one device holds (pages i * 12 to (i + 1) * 12 - 1), at most 3 go to one group, and every draw has a device that sends exactly 3 to some group.
All inputs are finite; a program needn't handle non-finite values.
Results may differ from a plain program's by a relative error of at most 0.009.
Values may be sent and summed in bfloat16 or wider, within the bound.
No kernel may reach another device: no remote copies, remote signals or barrier semaphores. Data moves between devices by JAX's collectives and lax.ppermute only.
A program may use at most 128 MiB of HBM per device.

v0:
```python
import jax
import jax.numpy as jnp
from jax import lax
from jax.sharding import PartitionSpec as P

D = 4096
HQ = 32
KVH = 8
HD = 128
TOPK = 2
PAGE = 64
REQS = 16
NEG_FILL = -1e30
EPSILON = 1e-05
HIGHEST = lax.Precision.HIGHEST


def joined(array, axis, combine):
    everything = jax.tree.map(lambda part: lax.all_gather(part, axis), array)
    initial = jax.tree.map(lambda part: part[0], everything)

    def hop(k, so_far):
        return combine(so_far, jax.tree.map(lambda part: part[k], everything))

    return lax.fori_loop(1, lax.axis_size(axis), hop, initial)


def gate_mix(logits, picked):
    expert_ids = jnp.arange(logits.shape[1], dtype=jnp.int32)[None, :]
    first_hit = picked[:, 0:1] == expert_ids
    second_hit = picked[:, 1:2] == expert_ids
    first_logit = jnp.sum(jnp.where(first_hit, logits, 0.0), axis=1)
    second_logit = jnp.sum(jnp.where(second_hit, logits, 0.0), axis=1)
    leading = 1.0 / (1.0 + jnp.exp(second_logit - first_logit))
    trailing = 1.0 / (1.0 + jnp.exp(first_logit - second_logit))
    return jnp.where(first_hit, leading[:, None], 0.0) + jnp.where(
        second_hit, trailing[:, None], 0.0
    )


def combine(earlier, later):
    first_top, first_sum, first_acc = earlier
    second_top, second_sum, second_acc = later
    joint_top = jnp.maximum(first_top, second_top)
    first_factor = jnp.exp(first_top - joint_top)
    second_factor = jnp.exp(second_top - joint_top)
    return (
        joint_top,
        first_sum * first_factor + second_sum * second_factor,
        first_acc * first_factor[..., None] + second_acc * second_factor[..., None],
    )


def slot_plan(page_dest, pages_dev, slot_count, slots_dev, replicas, groups):
    part_index = page_dest // slot_count
    within = page_dest % slot_count
    target = within // slots_dev * replicas + part_index
    position = within % slots_dev
    per_device = target.reshape(-1, pages_dev)
    onehot = (per_device[:, :, None] == jnp.arange(groups, dtype=jnp.int32)[None, None, :]).astype(
        jnp.int32
    )
    before = jnp.cumsum(onehot, axis=1) - onehot
    ranking = jnp.sum(before * onehot, axis=2).reshape(-1)
    return (target, position, ranking)


def partial_attention(page_block, owners, page_pos, lengths, grouped, score_scale):
    head_dim = grouped.shape[-1]
    page_len = page_block.shape[2]
    requests = grouped.shape[1]
    clipped = jnp.minimum(owners, requests - 1)
    length_cap = jnp.take(lengths, clipped)
    offsets = page_pos[:, None] * page_len + jnp.arange(page_len, dtype=jnp.int32)[None, :]
    is_live = (owners < requests)[:, None] & (offsets < length_cap[:, None])
    live_mask = is_live[None, :, None, None, :]
    asked_rows = jnp.take(grouped, clipped, axis=1)
    scores = (
        jnp.einsum(
            "spkgd,pktd->spkgt",
            asked_rows,
            page_block[..., :head_dim],
            preferred_element_type=jnp.float32,
        )
        * score_scale
    )
    scores = jnp.where(live_mask, scores, NEG_FILL)
    members = owners[:, None] == jnp.arange(requests, dtype=jnp.int32)[None, :]
    page_top = jnp.max(scores, axis=4)
    row_top = jnp.max(
        jnp.where(members[None, :, :, None, None], page_top[:, :, None], NEG_FILL), axis=1
    )
    weights = jnp.where(
        live_mask, jnp.exp(scores - jnp.take(row_top, clipped, axis=1)[..., None]), 0.0
    )
    member_mask = members.astype(jnp.float32)
    totals = jnp.einsum("pr,spkg->srkg", member_mask, jnp.sum(weights, axis=4), precision=HIGHEST)
    page_out = jnp.einsum(
        "spkgt,pktd->spkgd",
        weights.astype(jnp.bfloat16),
        page_block[..., head_dim:],
        preferred_element_type=jnp.float32,
    )
    weighted = jnp.einsum("pr,spkgd->srkgd", member_mask, page_out, precision=HIGHEST)
    return (row_top, totals, weighted)


def body(
    lengths,
    page_owner,
    page_index,
    page_dest,
    src_cache,
    queries,
    new_kv,
    hidden_in,
    out_weight,
    norm_gain,
    router,
    routes,
    w_gate,
    w_up,
    w_down,
):
    seq_count = lax.axis_size("seq")
    head_count = lax.axis_size("head")
    device_count = seq_count * head_count
    seq_pos = lax.axis_index("seq")
    head_pos = lax.axis_index("head")
    pages_dev = src_cache.shape[0]
    page_total = page_dest.shape[0]
    replicas = head_count // KVH
    groups = seq_count * replicas
    slot_count = page_total // replicas
    slots_dev = pages_dev * KVH
    capacity = (slots_dev + device_count - 1) // device_count
    group_size = HQ // KVH
    step_count = queries.shape[0]
    row_count = step_count * REQS
    source = seq_pos * head_count + head_pos
    target, position, ranking = slot_plan(
        page_dest, pages_dev, slot_count, slots_dev, replicas, groups
    )
    local_target = lax.dynamic_slice_in_dim(target, source * pages_dev, pages_dev)
    local_rank = lax.dynamic_slice_in_dim(ranking, source * pages_dev, pages_dev)
    wanted = jnp.arange(groups * capacity, dtype=jnp.int32)
    matches = (local_target[None, :] == (wanted // capacity)[:, None]) & (
        local_rank[None, :] == (wanted % capacity)[:, None]
    )
    picked_page = jnp.sum(
        jnp.where(matches, jnp.arange(pages_dev, dtype=jnp.int32)[None, :], 0), axis=1
    )
    filled = jnp.any(matches, axis=1)
    packed = jnp.where(
        filled[:, None, None, None],
        jnp.take(src_cache, picked_page, axis=0),
        jnp.zeros((), jnp.bfloat16),
    )
    packed = packed.reshape(seq_count, replicas, capacity, KVH, PAGE, 2 * HD).transpose(
        0, 3, 1, 2, 4, 5
    )
    arrived = lax.all_to_all(
        packed.reshape(device_count, capacity, PAGE, 2 * HD),
        ("seq", "head"),
        split_axis=0,
        concat_axis=0,
        tiled=True,
    )
    arrived = arrived.reshape(device_count * capacity, PAGE, 2 * HD)
    my_group = seq_pos * replicas + head_pos % replicas
    slot_ids = jnp.arange(slots_dev, dtype=jnp.int32)
    holders = (target[None, :] == my_group) & (position[None, :] == slot_ids[:, None])
    flat_index = jnp.arange(page_total, dtype=jnp.int32) // pages_dev * capacity + ranking
    chosen = jnp.sum(jnp.where(holders, flat_index[None, :], 0), axis=1)
    page_pool = jnp.take(arrived, chosen, axis=0)
    grouped = queries.reshape(step_count, REQS, KVH, group_size, HD)
    score_scale = HD ** (-0.5)
    owners = lax.dynamic_slice_in_dim(page_owner, source * pages_dev, pages_dev)
    places = lax.dynamic_slice_in_dim(page_index, source * pages_dev, pages_dev)
    row_top, totals, weighted = partial_attention(
        src_cache, owners, places, lengths, grouped, score_scale
    )
    row_top, totals, weighted = joined(
        (
            row_top.reshape(step_count, REQS, HQ),
            totals.reshape(step_count, REQS, HQ),
            weighted.reshape(step_count, REQS, HQ, HD),
        ),
        ("seq", "head"),
        combine,
    )
    fresh_scores = (
        jnp.einsum(
            "srkgd,urkd->srkgu", grouped, new_kv[..., :HD], preferred_element_type=jnp.float32
        )
        * score_scale
    )
    causal = (jnp.arange(step_count)[:, None] >= jnp.arange(step_count)[None, :])[:, None, None, :]
    fresh_scores = jnp.where(
        causal, fresh_scores.reshape(step_count, REQS, HQ, step_count), NEG_FILL
    )
    joint_top = jnp.maximum(row_top, jnp.max(fresh_scores, axis=3))
    factor = jnp.exp(row_top - joint_top)
    fresh_weights = jnp.where(causal, jnp.exp(fresh_scores - joint_top[..., None]), 0.0)
    totals = totals * factor + jnp.sum(fresh_weights, axis=3)
    fresh_rounded = fresh_weights.reshape(step_count, REQS, KVH, group_size, step_count).astype(
        jnp.bfloat16
    )
    fresh_out = jnp.einsum(
        "srkgu,urkd->srkgd", fresh_rounded, new_kv[..., HD:], preferred_element_type=jnp.float32
    )
    weighted = weighted * factor[..., None] + fresh_out.reshape(step_count, REQS, HQ, HD)
    attended = (weighted / totals[..., None]).reshape(row_count, HQ * HD).astype(jnp.bfloat16)
    attn_out = jnp.dot(attended, out_weight, preferred_element_type=jnp.float32)
    middle = hidden_in.reshape(row_count, -1).astype(jnp.float32) + attn_out
    gain_row = norm_gain.astype(jnp.float32)[None, :]
    squares, routed = lax.psum(
        (
            jnp.sum(middle * middle, axis=1),
            jnp.dot(middle * gain_row, router.astype(jnp.float32), precision=HIGHEST),
        ),
        ("seq", "head"),
    )
    inverse_rms = lax.rsqrt(squares / D + EPSILON)
    logits = routed * inverse_rms[:, None]
    normed = (middle * inverse_rms[:, None] * gain_row).astype(jnp.bfloat16)
    features = lax.all_gather(normed, ("seq", "head"), axis=1, tiled=True)
    mixture = gate_mix(logits, routes.reshape(row_count, TOPK))
    local_experts = w_gate.shape[0]
    local_mix = lax.dynamic_slice_in_dim(mixture, seq_pos * local_experts, local_experts, axis=1)
    gate_act = jnp.einsum("rd,edf->erf", features, w_gate, preferred_element_type=jnp.float32)
    upward = jnp.einsum("rd,edf->erf", features, w_up, preferred_element_type=jnp.float32)
    inner_act = (jax.nn.silu(gate_act) * upward).astype(jnp.bfloat16)
    produced = jnp.einsum("erf,efd->erd", inner_act, w_down, preferred_element_type=jnp.float32)
    moe_out = lax.psum_scatter(
        jnp.sum(local_mix.T[:, :, None] * produced, axis=0).T,
        ("seq", "head"),
        scatter_dimension=0,
        tiled=True,
    )
    mixed = (middle + moe_out.T).astype(jnp.bfloat16).reshape(step_count, REQS, -1)
    return (page_pool[None], mixed)


def solution(mesh):
    in_specs = (
        P(),
        P(),
        P(),
        P(),
        P(("seq", "head"), None, None, None),
        P(),
        P(),
        P(None, None, ("seq", "head")),
        P(None, ("seq", "head")),
        P(("seq", "head")),
        P(("seq", "head"), None),
        P(),
        P("seq", None, "head"),
        P("seq", None, "head"),
        P("seq", "head", None),
    )
    out_specs = (P("head", "seq", None, None), P(None, None, ("seq", "head")))
    return jax.shard_map(body, mesh=mesh, in_specs=in_specs, out_specs=out_specs, check_vma=False)
```

profile of v0, /device:TPU:0, one launch (start us, length us, event | category | flops | bytes accessed | tf_op | source)
XLA Modules:
  0.0 518.8 jit_solution(1423229279083668692)
XLA Ops:
  7.2 0.8 broadcast_compare_fusion.1
  8.1 1.1 reshape.265
  9.3 1.3 gather_fusion.2
  10.6 0.6 gather_fusion.3
  11.2 0.8 dynamic-slice_multiply_fusion
  12.1 2.5 fusion.75
  15.2 0.6 gather_fusion.4
  16.1 2.0 fusion.10
  18.1 0.7 fusion.29
  18.8 0.9 copy.114
  20.7 4.4 gather_fusion
  25.4 2.3 select_bitcast_fusion
  27.7 2.1 copy.100
  29.8 7.4 %all-to-all-start = ((bf16[32,3,64,256]{3,2,1,0:T(8,128)(2,1)}), bf16[32,3,64,256]{3,2,1,0:T(8,128)(2,1)}, u32[]{:S(2)}, u32[]{:S(2)}) async-start(bf16[32,3,64,256]{3,2,1,0:T(8,128)(2,1)} %bitcast.150), calls=%async_computation | async-start | bytes 6291456 | tf_op jit(solution)/shard_map/all_to_all | solution.py:162
  37.3 0.6 fusion.38
  38.5 2.4 fusion.76
  41.2 115.7 %all_gather.13 = f32[32,2,16,32]{3,2,1,0:T(8,128)S(1)} all-gather(f32[1,2,16,32]{3,2,1,0:T(8,128)S(1)} %copy.112), channel_id=1, replica_groups=mesh['seq'=4,'head'=8] {'seq','head'}, dimensions={0}, use_global_device_ids=true | all-gather | bytes 135168 | tf_op jit(solution)/shard_map/all_gather | solution.py:19
  156.9 68.5 %all_gather.12 = f32[32,2,16,32]{3,2,1,0:T(8,128)S(1)} all-gather(f32[1,2,16,32]{3,2,1,0:T(8,128)S(1)} %copy.106), channel_id=1, replica_groups=mesh['seq'=4,'head'=8] {'seq','head'}, dimensions={0}, use_global_device_ids=true | all-gather | bytes 135168 | tf_op jit(solution)/shard_map/all_gather | solution.py:19
  225.5 1.1 slice_bitcast_fusion
  226.6 49.5 %while.19 = (s32[]{:T(128)}, f32[2,16,32]{2,1,0:T(8,128)S(1)}, f32[2,16,32]{2,1,0:T(8,128)S(1)}, f32[2,16,32,128]{3,2,1,0:T(8,128)S(1)}, f32[32,2,16,32]{3,2,1,0...) while((s32[]{:T(128)}, f32[2,16,32]{2,1,0:T(8,128)S(1)}, ...), condition=%wide.region_9.10_spmd, body=%wide.region_8.9_spmd.sunk | while | flops 399365 | bytes 1613975 | solution.py:25
  226.6 1.5 fusion.87
  228.2 1.5 fusion.87
  229.8 1.5 fusion.87
  231.4 1.5 fusion.87
  233.0 1.5 fusion.87
  234.6 1.5 fusion.87
  236.2 1.5 fusion.87
  237.8 1.5 fusion.87
  239.4 1.5 fusion.87
  241.0 1.5 fusion.87
  242.6 1.5 fusion.87
  244.2 1.5 fusion.87
  245.8 1.5 fusion.87
  247.4 1.5 fusion.87
  249.0 1.5 fusion.87
  250.6 1.5 fusion.87
  252.2 1.5 fusion.87
  253.8 1.5 fusion.87
  255.4 1.5 fusion.87
  257.0 1.5 fusion.87
  258.6 1.5 fusion.87
  260.2 1.5 fusion.87
  261.8 1.5 fusion.87
  263.4 1.5 fusion.87
  265.0 1.5 fusion.87
  266.6 1.5 fusion.87
  268.2 1.5 fusion.87
  269.8 1.5 fusion.87
  271.4 1.5 fusion.87
  273.0 1.5 fusion.87
  274.6 1.5 fusion.87
  276.4 0.6 fusion.51
  277.3 0.5 convolution_bitcast_fusion
  278.1 0.4 fusion.31
  278.6 0.4 multiply_reduce_fusion
  279.1 36.9 %all-reduce = (f32[32]{0:T(128)S(1)}, f32[32,8]{0,1:T(8,128)S(1)}) all-reduce(f32[32]{0:T(128)S(1)} %get-tuple-element.237, f32[32,8]{0,1:T(8,128)S(1)} %fusion.48), channel_id=1, replica_groups=mesh['seq'=4,'head'=8] {'seq','head'}, use_global_device_ids=true, to_apply=%region_14.15 | all-reduce | flops 288 | bytes 2304 | tf_op jit(solution)/shard_map/psum | solution.py:217
  316.1 41.0 %all_gather.15 = bf16[32,4096]{1,0:T(8,128)(2,1)S(1)} all-gather(bf16[32,128]{1,0:T(8,128)(2,1)S(1)} %multiply_convert_fusion), channel_id=1, replica_groups=mesh['seq'=4,'head'=8] {'seq','head'}, dimensions={1}, use_global_device_ids=true | all-gather | bytes 270336 | tf_op jit(solution)/shard_map/all_gather | solution.py:227
  357.2 8.9 %convolution_bitcast_fusion.2 = f32[2,32,1024]{2,1,0:T(8,128)S(1)} fusion(bf16[2,4096,1024]{2,1,0:T(8,128)(2,1)} %param.29, bf16[32,4096]{1,0:T(8,128)(2,1)S(1)} %all_gather.15), kind=kOutput, calls=%fused_computation.30 | convolution fusion | flops 536870912 | bytes 17301504 | tf_op jit(solution)/shard_map/rd,edf->erf/dot_general | solution.py:231
  366.1 8.9 %fusion.25 = bf16[2,32,1024]{2,1,0:T(8,128)(2,1)S(1)} fusion(bf16[2,4096,1024]{2,1,0:T(8,128)(2,1)} %param.30, bf16[32,4096]{1,0:T(8,128)(2,1)S(1)} %all_gather.15, f32[2,32,1024]{2,1,0:T(8,128)S(1)} %convolution_bitcast_fusion.2), kind=kOutput, calls=%fused_computation.34 | convolution fusion | flops 537264128 | bytes 17432576 | tf_op jit(solution)/shard_map/rd,edf->erf/dot_general | solution.py:232
  375.1 3.8 fusion.9
  379.0 4.5 gather_fusion.1
  383.6 3.9 bitcast_select_fusion
  387.5 123.2 %reduce-scatter.2.cloned.1.call-done = f32[128,32]{0,1:T(8,128)} async-done(((f32[4096,32]{0,1:T(8,128)}), f32[128,32]{0,1:T(8,128)}) %reduce-scatter.2.cloned.1.call-update) | async-done | bytes 16400 | tf_op jit(solution)/shard_map/reduce_scatter | solution.py:235
  510.7 1.3 fusion.47
  (125 shorter events, 5.3 us)
Async XLA Ops:
  7.2 271.4 %copy-start = (bf16[4096,128]{1,0:T(8,128)(2,1)S(1)}, bf16[4096,128]{1,0:T(8,128)(2,1)}, u32[]{:S(2)}) copy-start(bf16[4096,128]{1,0:T(8,128)(2,1)} %param.25) | copy-start | bytes 3145732
  7.2 218.3 %all-gather.2.cloned.1.call-start = ((), (), s32[]{:S(2)}) async-start(), calls=%async_computation.2 | async-start | bytes 17301504 | tf_op jit(solution)/shard_map/all_gather | solution.py:19
  16.1 3.7 copy-start.4
  29.8 8.7 %copy-start.2 = (bf16[2,16,8,256]{3,2,1,0:T(8,128)(2,1)S(1)}, bf16[2,16,8,256]{3,2,1,0:T(8,128)(2,1)}, u32[]{:S(2)}) copy-start(bf16[2,16,8,256]{3,2,1,0:T(8,128)(2,1)} %param.23) | copy-start | bytes 393220
  29.8 349.2 %all-to-all-start = ((bf16[32,3,64,256]{3,2,1,0:T(8,128)(2,1)}), bf16[32,3,64,256]{3,2,1,0:T(8,128)(2,1)}, u32[]{:S(2)}, u32[]{:S(2)}) async-start(bf16[32,3,64,256]{3,2,1,0:T(8,128)(2,1)} %bitcast.150), calls=%async_computation | async-start | bytes 6291456 | tf_op jit(solution)/shard_map/all_to_all | solution.py:162
  37.2 3.9 copy-start.7
  37.2 3.9 copy-start.6
  37.2 473.4 %reduce-scatter.2.cloned.1.call-start = ((), (), s32[]{:S(2)}) async-start(), calls=%async_computation.3 | async-start | bytes 540672 | tf_op jit(solution)/shard_map/reduce_scatter | solution.py:235
  276.1 2.4 copy-start.3
  277.0 2.0 copy-start.5
  357.2 17.8 %slice-start = ((s8[16777216]{0:T(1024)(128)(4,1)}), s8[4194304]{0:T(1024)(128)(4,1)S(1)}, s32[]{:S(2)}) async-start(s8[16777216]{0:T(1024)(128)(4,1)} %bitcast.148), calls=%async_computation.4 | async-start | bytes 8388608
  357.2 17.8 %slice-start.1 = ((s8[16777216]{0:T(1024)(128)(4,1)}), s8[4194304]{0:T(1024)(128)(4,1)S(1)}, s32[]{:S(2)}) async-start(s8[16777216]{0:T(1024)(128)(4,1)} %bitcast.148), calls=%async_computation.5 | async-start | bytes 8388608
  366.1 9.0 %slice-start.2 = ((s8[16777216]{0:T(1024)(128)(4,1)}), s8[4194304]{0:T(1024)(128)(4,1)S(1)}, s32[]{:S(2)}) async-start(s8[16777216]{0:T(1024)(128)(4,1)} %bitcast.148), calls=%async_computation.6 | async-start | bytes 8388608
  366.1 9.0 %slice-start.3 = ((s8[16777216]{0:T(1024)(128)(4,1)}), s8[4194304]{0:T(1024)(128)(4,1)S(1)}, s32[]{:S(2)}) async-start(s8[16777216]{0:T(1024)(128)(4,1)} %bitcast.148), calls=%async_computation.7 | async-start | bytes 8388608
  379.0 132.9 %copy-start.1 = (bf16[4096,128]{1,0:T(8,128)(2,1)S(1)}, bf16[4096,128]{1,0:T(8,128)(2,1)}, u32[]{:S(2)}) copy-start(bf16[4096,128]{1,0:T(8,128)(2,1)} %param.25) | copy-start | bytes 3145732
Sparse Core Ops, SparseCore 0:
  19.9 166.8 all-gather.1
  379.0 131.6 reduce-scatter.1
where the time goes:
time: 521 us; the launch traced here: 519 us
  blocking collectives  262 us (50%)
  waiting for transfers between devices  123 us (24%)
  other arithmetic  60.5 us (12%)
  matrix products  30.4 us (6%)
  local copies, waits for them, and re-layouts  19.7 us (4%)
  between operations  14.5 us (3%)
  starting transfers between devices  7.51 us (1%)
    all_gather x2, blocking collectives, joined(): everything = jax.tree.map(lambda part: lax.all_gather(part, axis), array)  184 us
    reduce_scatter x1, waiting for transfers between devices, body(): lax.psum_scatter(jnp.sum(local_mix.T[:, :, None] * produced, axis=0).T, (...  123 us
    add x31, other arithmetic, combine(): first_acc * first_factor[..., None] + second_acc * second_factor[..., None]  47.9 us
    all_gather x1, blocking collectives, body(): features = lax.all_gather(normed, ('seq', 'head'), axis=1, tiled=True)  41 us
    psum x1, blocking collectives, body(): lax.psum((jnp.sum(middle * middle, axis=1), jnp.dot(middle * gain_row, ro...  36.9 us
  transfers between devices with their start and end apart: 3, of which 1 were waited for; matrix products, arithmetic and copies ran while one was open for 19% of the time, Pallas kernels for 0%

commit v1 on v0

--- a/solution.py
+++ b/solution.py
@@ -13,6 +13,11 @@
 NEG_FILL = -1e30
 EPSILON = 1e-05
 HIGHEST = lax.Precision.HIGHEST
+
+
+def axis_by_axis(array_2, inner_axis, outer_axis):
+    inner = lax.psum(array_2, inner_axis)
+    return lax.psum(inner, outer_axis)
 
 
 def joined(array, axis, combine):
@@ -214,12 +219,13 @@
     attn_out = jnp.dot(attended, out_weight, preferred_element_type=jnp.float32)
     middle = hidden_in.reshape(row_count, -1).astype(jnp.float32) + attn_out
     gain_row = norm_gain.astype(jnp.float32)[None, :]
-    squares, routed = lax.psum(
+    squares, routed = axis_by_axis(
         (
             jnp.sum(middle * middle, axis=1),
             jnp.dot(middle * gain_row, router.astype(jnp.float32), precision=HIGHEST),
         ),
-        ("seq", "head"),
+        "head",
+        "seq",
     )
     inverse_rms = lax.rsqrt(squares / D + EPSILON)
     logits = routed * inverse_rms[:, None]

time: 521 us -> 503 us (0.965)
  blocking collectives: 262 us -> 243 us
    psum x1 -> x2, blocking collectives: 36.9 us -> 20.9 us  [the longest x1 12.4 us: axis_by_axis(): inner = lax.psum(array_2, inner_axis)]
where the time goes in v1:
time: 503 us; the launch traced here: 501 us
  blocking collectives  243 us (48%)
  waiting for transfers between devices  125 us (25%)
  other arithmetic  60.5 us (12%)
  matrix products  30.4 us (6%)
  local copies, waits for them, and re-layouts  19.7 us (4%)
  between operations  14.5 us (3%)
  starting transfers between devices  7.51 us (1%)
    all_gather x2, blocking collectives, joined(): everything = jax.tree.map(lambda part: lax.all_gather(part, axis), array)  184 us
    reduce_scatter x1, waiting for transfers between devices, body(): lax.psum_scatter(jnp.sum(local_mix.T[:, :, None] * produced, axis=0).T, (...  125 us
    add x31, other arithmetic, combine(): first_acc * first_factor[..., None] + second_acc * second_factor[..., None]  47.9 us
    all_gather x1, blocking collectives, body(): features = lax.all_gather(normed, ('seq', 'head'), axis=1, tiled=True)  37.6 us
    psum x1, blocking collectives, axis_by_axis(): inner = lax.psum(array_2, inner_axis)  12.4 us
  transfers between devices with their start and end apart: 3, of which 1 were waited for; matrix products, arithmetic and copies ran while one was open for 19% of the time, Pallas kernels for 0%

profile of v1, /device:TPU:0, one launch (start us, length us, event | category | flops | bytes accessed | tf_op | source)
XLA Modules:
  0.0 500.9 jit_solution(17140045065388001763)
XLA Ops:
  7.2 0.8 broadcast_compare_fusion.1
  8.1 1.1 reshape.265
  9.3 1.3 gather_fusion.2
  10.6 0.6 gather_fusion.3
  11.2 0.8 dynamic-slice_multiply_fusion
  12.1 2.5 fusion.75
  15.2 0.6 gather_fusion.4
  16.1 2.0 fusion.10
  18.1 0.7 fusion.29
  18.8 0.9 copy.114
  20.7 4.4 gather_fusion
  25.4 2.3 select_bitcast_fusion
  27.7 2.1 copy.100
  29.8 7.4 %all-to-all-start = ((bf16[32,3,64,256]{3,2,1,0:T(8,128)(2,1)}), bf16[32,3,64,256]{3,2,1,0:T(8,128)(2,1)}, u32[]{:S(2)}, u32[]{:S(2)}) async-start(bf16[32,3,64,256]{3,2,1,0:T(8,128)(2,1)} %bitcast.150), calls=%async_computation | async-start | bytes 6291456 | tf_op jit(solution)/shard_map/all_to_all | solution.py:167
  37.3 0.6 fusion.38
  38.5 2.4 fusion.76
  41.2 115.7 %all_gather.13 = f32[32,2,16,32]{3,2,1,0:T(8,128)S(1)} all-gather(f32[1,2,16,32]{3,2,1,0:T(8,128)S(1)} %copy.112), channel_id=1, replica_groups=mesh['seq'=4,'head'=8] {'seq','head'}, dimensions={0}, use_global_device_ids=true | all-gather | bytes 135168 | tf_op jit(solution)/shard_map/all_gather | solution.py:24
  156.9 68.5 %all_gather.12 = f32[32,2,16,32]{3,2,1,0:T(8,128)S(1)} all-gather(f32[1,2,16,32]{3,2,1,0:T(8,128)S(1)} %copy.106), channel_id=1, replica_groups=mesh['seq'=4,'head'=8] {'seq','head'}, dimensions={0}, use_global_device_ids=true | all-gather | bytes 135168 | tf_op jit(solution)/shard_map/all_gather | solution.py:24
  225.5 1.1 slice_bitcast_fusion
  226.6 49.5 %while.19 = (s32[]{:T(128)}, f32[2,16,32]{2,1,0:T(8,128)S(1)}, f32[2,16,32]{2,1,0:T(8,128)S(1)}, f32[2,16,32,128]{3,2,1,0:T(8,128)S(1)}, f32[32,2,16,32]{3,2,1,0...) while((s32[]{:T(128)}, f32[2,16,32]{2,1,0:T(8,128)S(1)}, ...), condition=%wide.region_9.10_spmd, body=%wide.region_8.9_spmd.sunk | while | flops 399365 | bytes 1613975 | solution.py:30
  226.6 1.5 fusion.87
  228.2 1.5 fusion.87
  229.8 1.5 fusion.87
  231.4 1.5 fusion.87
  233.0 1.5 fusion.87
  234.6 1.5 fusion.87
  236.2 1.5 fusion.87
  237.8 1.5 fusion.87
  239.4 1.5 fusion.87
  241.0 1.5 fusion.87
  242.6 1.5 fusion.87
  244.2 1.5 fusion.87
  245.8 1.5 fusion.87
  247.4 1.5 fusion.87
  249.0 1.5 fusion.87
  250.6 1.5 fusion.87
  252.2 1.5 fusion.87
  253.8 1.5 fusion.87
  255.4 1.5 fusion.87
  257.0 1.5 fusion.87
  258.6 1.5 fusion.87
  260.2 1.5 fusion.87
  261.8 1.5 fusion.87
  263.4 1.5 fusion.87
  265.0 1.5 fusion.87
  266.6 1.5 fusion.87
  268.2 1.5 fusion.87
  269.8 1.5 fusion.87
  271.4 1.5 fusion.87
  273.0 1.5 fusion.87
  274.6 1.5 fusion.87
  276.4 0.6 fusion.51
  277.3 0.5 convolution_bitcast_fusion
  278.6 0.4 multiply_reduce_fusion
  279.1 12.4 %all-reduce = (f32[32]{0:T(128)S(1)}, f32[32,8]{0,1:T(8,128)S(1)}) all-reduce(f32[32]{0:T(128)S(1)} %get-tuple-element.239, f32[32,8]{0,1:T(8,128)S(1)} %fusion.48), channel_id=1, replica_groups=mesh['seq'=4,'head'=8] {'head'}, use_global_device_ids=true, to_apply=%region_15.16 | all-reduce | flops 288 | bytes 2304 | tf_op jit(solution)/shard_map/psum | solution.py:19
  291.5 8.5 %all-reduce.1 = (f32[32]{0:T(128)S(1)}, f32[32,8]{0,1:T(8,128)S(1)}) all-reduce(f32[32]{0:T(128)S(1)} %get-tuple-element.213, f32[32,8]{0,1:T(8,128)S(1)} %get-tuple-element.214), channel_id=1, replica_groups=mesh['seq'=4,'head'=8] {'seq'}, use_global_device_ids=true, to_apply=%region_16.17 | all-reduce | flops 288 | bytes 2304 | tf_op jit(solution)/shard_map/psum | solution.py:20
  300.2 37.6 %all_gather.15 = bf16[32,4096]{1,0:T(8,128)(2,1)S(1)} all-gather(bf16[32,128]{1,0:T(8,128)(2,1)S(1)} %multiply_convert_fusion), channel_id=1, replica_groups=mesh['seq'=4,'head'=8] {'seq','head'}, dimensions={1}, use_global_device_ids=true | all-gather | bytes 270336 | tf_op jit(solution)/shard_map/all_gather | solution.py:233
  337.8 8.9 %convolution_bitcast_fusion.2 = f32[2,32,1024]{2,1,0:T(8,128)S(1)} fusion(bf16[2,4096,1024]{2,1,0:T(8,128)(2,1)} %param.29, bf16[32,4096]{1,0:T(8,128)(2,1)S(1)} %all_gather.15), kind=kOutput, calls=%fused_computation.30 | convolution fusion | flops 536870912 | bytes 17301504 | tf_op jit(solution)/shard_map/rd,edf->erf/dot_general | solution.py:237
  346.7 8.9 %fusion.25 = bf16[2,32,1024]{2,1,0:T(8,128)(2,1)S(1)} fusion(bf16[2,4096,1024]{2,1,0:T(8,128)(2,1)} %param.30, bf16[32,4096]{1,0:T(8,128)(2,1)S(1)} %all_gather.15, f32[2,32,1024]{2,1,0:T(8,128)S(1)} %convolution_bitcast_fusion.2), kind=kOutput, calls=%fused_computation.34 | convolution fusion | flops 537264128 | bytes 17432576 | tf_op jit(solution)/shard_map/rd,edf->erf/dot_general | solution.py:238
  355.7 3.8 fusion.9
  359.7 4.5 gather_fusion.1
  364.2 3.9 bitcast_select_fusion
  368.1 124.6 %reduce-scatter.2.cloned.1.call-done = f32[128,32]{0,1:T(8,128)} async-done(((f32[4096,32]{0,1:T(8,128)}), f32[128,32]{0,1:T(8,128)}) %reduce-scatter.2.cloned.1.call-update) | async-done | bytes 16400 | tf_op jit(solution)/shard_map/reduce_scatter | solution.py:241
  492.7 1.3 fusion.47
  (126 shorter events, 5.8 us)
Async XLA Ops:
  7.2 271.4 %copy-start = (bf16[4096,128]{1,0:T(8,128)(2,1)S(1)}, bf16[4096,128]{1,0:T(8,128)(2,1)}, u32[]{:S(2)}) copy-start(bf16[4096,128]{1,0:T(8,128)(2,1)} %param.25) | copy-start | bytes 3145732
  7.2 218.3 %all-gather.2.cloned.1.call-start = ((), (), s32[]{:S(2)}) async-start(), calls=%async_computation.2 | async-start | bytes 17301504 | tf_op jit(solution)/shard_map/all_gather | solution.py:24
  16.1 3.7 copy-start.4
  29.8 8.7 %copy-start.2 = (bf16[2,16,8,256]{3,2,1,0:T(8,128)(2,1)S(1)}, bf16[2,16,8,256]{3,2,1,0:T(8,128)(2,1)}, u32[]{:S(2)}) copy-start(bf16[2,16,8,256]{3,2,1,0:T(8,128)(2,1)} %param.23) | copy-start | bytes 393220
  29.8 329.9 %all-to-all-start = ((bf16[32,3,64,256]{3,2,1,0:T(8,128)(2,1)}), bf16[32,3,64,256]{3,2,1,0:T(8,128)(2,1)}, u32[]{:S(2)}, u32[]{:S(2)}) async-start(bf16[32,3,64,256]{3,2,1,0:T(8,128)(2,1)} %bitcast.150), calls=%async_computation | async-start | bytes 6291456 | tf_op jit(solution)/shard_map/all_to_all | solution.py:167
  37.2 3.9 copy-start.7
  37.2 3.9 copy-start.6
  37.2 455.5 %reduce-scatter.2.cloned.1.call-start = ((), (), s32[]{:S(2)}) async-start(), calls=%async_computation.3 | async-start | bytes 540672 | tf_op jit(solution)/shard_map/reduce_scatter | solution.py:241
  276.1 2.4 copy-start.3
  277.0 2.0 copy-start.5
  337.8 17.8 %slice-start = ((s8[16777216]{0:T(1024)(128)(4,1)}), s8[4194304]{0:T(1024)(128)(4,1)S(1)}, s32[]{:S(2)}) async-start(s8[16777216]{0:T(1024)(128)(4,1)} %bitcast.148), calls=%async_computation.4 | async-start | bytes 8388608
  337.8 17.8 %slice-start.1 = ((s8[16777216]{0:T(1024)(128)(4,1)}), s8[4194304]{0:T(1024)(128)(4,1)S(1)}, s32[]{:S(2)}) async-start(s8[16777216]{0:T(1024)(128)(4,1)} %bitcast.148), calls=%async_computation.5 | async-start | bytes 8388608
  346.7 9.0 %slice-start.2 = ((s8[16777216]{0:T(1024)(128)(4,1)}), s8[4194304]{0:T(1024)(128)(4,1)S(1)}, s32[]{:S(2)}) async-start(s8[16777216]{0:T(1024)(128)(4,1)} %bitcast.148), calls=%async_computation.6 | async-start | bytes 8388608
  346.7 9.0 %slice-start.3 = ((s8[16777216]{0:T(1024)(128)(4,1)}), s8[4194304]{0:T(1024)(128)(4,1)S(1)}, s32[]{:S(2)}) async-start(s8[16777216]{0:T(1024)(128)(4,1)} %bitcast.148), calls=%async_computation.7 | async-start | bytes 8388608
  359.7 134.4 %copy-start.1 = (bf16[4096,128]{1,0:T(8,128)(2,1)S(1)}, bf16[4096,128]{1,0:T(8,128)(2,1)}, u32[]{:S(2)}) copy-start(bf16[4096,128]{1,0:T(8,128)(2,1)} %param.25) | copy-start | bytes 3145732
Sparse Core Ops, SparseCore 0:
  19.9 166.8 all-gather.1
  359.6 133.0 reduce-scatter.1
